TPU v7x, 32 devices: a whole 2x2x4 slice. The times are simulated.
32 devices in a mesh: row: 8 (over z, core), col: 4 (over y, x).
Axes of the slice: x: 2, y: 2, z: 4, core: 2. Of those that a mesh axis runs over, the one named last changes fastest.
Arguments:
- points: bfloat16 [2048, 1024], P(('row', 'col')), may hold values from -6 to 6
- factor: float32 [2048, 256], P(('row', 'col')), may hold values from 0 to 1
Outputs:
- factor_out: float32 [2048, 256], P(('row', 'col'))
All inputs are finite; a program needn't handle non-finite values.
Results may differ from a plain program's by a relative error of at most 0.002.
The roundings to bfloat16 on the way count: a program that leaves them out, or rounds other values in their place, can miss the bound.
Values may be sent and summed in bfloat16 or wider, within the bound.
A program may use at most 64 MiB of HBM per device.

v0:
```python
import math
import jax
import jax.numpy as jnp
from jax import lax
from jax.sharding import PartitionSpec as P

EMBED_WIDTH = 1024
ITERS = 2


def shards(points, factor):
    nrow = lax.axis_size("row")
    ncol = lax.axis_size("col")
    pts = points.shape[0]
    rank = factor.shape[1]
    total = pts * nrow * ncol
    row_pts = lax.all_gather(points, "col", axis=0, tiled=True)
    col_pts = lax.all_gather(points, "row", axis=0, tiled=True)
    gram_matrix = lax.dot_general(
        row_pts, col_pts, (((1,), (1,)), ((), ())), preferred_element_type=jnp.float32
    )
    row_sq = jnp.sum(jnp.square(row_pts.astype(jnp.float32)), axis=1)
    col_sq = jnp.sum(jnp.square(col_pts.astype(jnp.float32)), axis=1)
    kern = jnp.exp((2.0 * gram_matrix - row_sq[:, None] - col_sq[None, :]) * (0.5 / EMBED_WIDTH))
    row_sum, band = lax.psum((jnp.sum(kern, axis=1), jnp.sum(kern)), "col")
    col_sum, grand = lax.psum((jnp.sum(kern, axis=0), band), "row")
    affinity = (
        kern - row_sum[:, None] / total - col_sum[None, :] / total + grand / (total * total)
    ).astype(jnp.bfloat16)
    unit = 2.0 / math.sqrt(total * rank)
    h = factor * unit
    for step in range(ITERS):
        hb = h.astype(jnp.bfloat16)
        copies = lax.all_gather(hb, "row", axis=0, tiled=True)
        ah = lax.psum_scatter(
            jnp.dot(affinity, copies, preferred_element_type=jnp.float32),
            "col",
            scatter_dimension=0,
            tiled=True,
        )
        local_gram = lax.dot_general(
            h, h, (((0,), (0,)), ((), ())), precision=lax.Precision.HIGHEST
        )
        hh = lax.psum(local_gram, ("row", "col"))
        scale = 0.5 / jnp.sqrt(jnp.sum(hh * hh) + 1e-06)
        h = jnp.maximum(h - scale * (jnp.dot(h, hh, precision=lax.Precision.HIGHEST) - ah), 0.0)
    return h / unit


def solution(mesh):
    in_specs = (P(("row", "col"), None), P(("row", "col"), None))
    out_specs = P(("row", "col"), None)
    return jax.shard_map(shards, mesh=mesh, in_specs=in_specs, out_specs=out_specs, check_vma=False)
```

profile of v0, /device:TPU:0, one launch (start us, length us, event | category | flops | bytes accessed | tf_op | source)
XLA Modules:
  0.0 301.0 jit_solution(7194826416192646812)
XLA Ops:
  7.4 0.0 all-gather.2.cloned.1.call-start
  7.4 0.7 all-gather.2.cloned.1.call-update
  8.1 0.0 all-reduce.5.cloned.1.call-start
  8.1 2.0 fusion.12
  10.2 0.0 all-reduce.5.cloned.1.call-update
  10.2 0.0 reduce-scatter.3.cloned.1.call-start
  10.3 11.9 %all_gather.12 = bf16[256,1024]{1,0:T(8,128)(2,1)S(1)} all-gather(bf16[64,1024]{1,0:T(8,128)(2,1)} %param.2), channel_id=1, replica_groups=mesh['row'=8,'col'=4] {'col'}, dimensions={0}, use_global_device_ids=true | all-gather | bytes 655360 | tf_op jit(solution)/shard_map/all_gather | solution.py:17
  22.1 0.0 copy-done.1
  22.2 0.2 multiply_reduce_fusion.1
  22.3 15.2 %all_gather.14 = bf16[512,256]{1,0:T(8,128)(2,1)S(1)} all-gather(bf16[64,256]{1,0:T(8,128)(2,1)S(1)} %multiply_convert_fusion), channel_id=1, replica_groups=mesh['row'=8,'col'=4] {'row'}, dimensions={0}, use_global_device_ids=true | all-gather | bytes 294912 | tf_op jit(solution)/shard_map/all_gather | solution.py:34
  37.6 1.6 multiply_reduce_fusion
  39.2 0.0 copy-done
  39.2 1.2 fusion.20
  40.4 9.6 %all-reduce.1 = (f32[]{:T(128)}, f32[256]{0:T(256)S(1)}) all-reduce(f32[]{:T(128)} %get-tuple-element.6, f32[256]{0:T(256)S(1)} %get-tuple-element.5), channel_id=1, replica_groups=mesh['row'=8,'col'=4] {'col'}, use_global_device_ids=true, to_apply=%region_9.0 | all-reduce | flops 257 | bytes 2056 | tf_op jit(solution)/shard_map/psum | solution.py:25
  50.0 15.4 %all-reduce = (f32[]{:T(128)}, f32[512]{0:T(512)S(1)}) all-reduce(f32[]{:T(128)} %get-tuple-element.10, f32[512]{0:T(512)S(1)} %get-tuple-element.7), channel_id=1, replica_groups=mesh['row'=8,'col'=4] {'row'}, use_global_device_ids=true, to_apply=%region_10.0 | all-reduce | flops 513 | bytes 4104 | tf_op jit(solution)/shard_map/psum | solution.py:26
  66.1 1.0 fusion.19
  67.1 0.0 reduce-scatter.3.cloned.1.call-update
  67.1 0.0 all-reduce.7.cloned.1.call-start
  67.2 78.5 %all-reduce.5.cloned.1.call-done = f32[256,256]{1,0:T(8,128)} async-done(((f32[256,256]{1,0:T(8,128)}), f32[256,256]{1,0:T(8,128)}) %all-reduce.5.cloned.1.call-update) | async-done | bytes 262160 | tf_op jit(solution)/shard_map/psum | solution.py:44
  145.6 1.6 multiply_reduce_fusion.3
  147.9 0.0 reduce-scatter.3.cloned.1.call-done
  148.0 1.2 fusion.21
  149.2 14.2 %all_gather.15 = bf16[512,256]{1,0:T(8,128)(2,1)S(1)} all-gather(bf16[64,256]{1,0:T(8,128)(2,1)S(1)} %get-tuple-element.13), channel_id=1, replica_groups=mesh['row'=8,'col'=4] {'row'}, dimensions={0}, use_global_device_ids=true | all-gather | bytes 294912 | tf_op jit(solution)/shard_map/all_gather | solution.py:34
  163.4 1.1 fusion.22
  164.5 0.0 all-reduce.7.cloned.1.call-update
  164.5 0.0 reduce-scatter.5.cloned.1.call-start
  164.6 1.0 fusion.18
  165.6 0.0 reduce-scatter.5.cloned.1.call-update
  165.6 124.1 %all-reduce.7.cloned.1.call-done = f32[256,256]{1,0:T(8,128)} async-done(((f32[256,256]{1,0:T(8,128)}), f32[256,256]{1,0:T(8,128)}) %all-reduce.7.cloned.1.call-update) | async-done | bytes 262160 | tf_op jit(solution)/shard_map/psum | solution.py:44
  289.7 1.6 multiply_reduce_fusion.2
  292.0 0.0 reduce-scatter.5.cloned.1.call-done
  292.0 1.8 fusion.7
  (6 shorter events, 0.0 us)
Async XLA Ops:
  7.4 14.8 %copy-start.1 = (f32[64,256]{1,0:T(8,128)S(1)}, f32[64,256]{1,0:T(8,128)}, u32[]{:S(2)}) copy-start(f32[64,256]{1,0:T(8,128)} %param.3) | copy-start | bytes 196612
  7.4 30.2 %all-gather.2.cloned.1.call-start = ((), (), s32[]{:S(2)}) async-start(), calls=%async_computation.3 | async-start | bytes 1179648 | tf_op jit(solution)/shard_map/all_gather | solution.py:18
  8.1 137.5 %all-reduce.5.cloned.1.call-start = ((), (), s32[]{:S(2)}) async-start(), calls=%async_computation.2 | async-start | bytes 524288 | tf_op jit(solution)/shard_map/psum | solution.py:44
  10.2 137.8 %reduce-scatter.3.cloned.1.call-start = ((), (), s32[]{:S(2)}) async-start(), calls=%async_computation.4 | async-start | bytes 327680 | tf_op jit(solution)/shard_map/reduce_scatter | solution.py:35
  37.6 1.6 copy-start
  67.1 222.6 %all-reduce.7.cloned.1.call-start = ((), (), s32[]{:S(2)}) async-start(), calls=%async_computation.5 | async-start | bytes 524288 | tf_op jit(solution)/shard_map/psum | solution.py:44
  164.5 127.5 %reduce-scatter.5.cloned.1.call-start = ((), (), s32[]{:S(2)}) async-start(), calls=%async_computation.6 | async-start | bytes 327680 | tf_op jit(solution)/shard_map/reduce_scatter | solution.py:35
Sparse Core Ops, SparseCore 0:
  9.8 26.2 all-gather.1
  67.2 21.1 reduce-scatter.2
  168.1 23.4 reduce-scatter.4
Sparse Core Ops, SparseCore 1:
  14.1 131.5 all-reduce.4
  164.6 125.0 all-reduce.6
where the time goes:
time: 301 us
  waiting for transfers between devices  203 us (67%)
  blocking collectives  66.4 us (22%)
  between operations  16.6 us (6%)
  matrix products  9.4 us (3%)
  other arithmetic  5.03 us (2%)
    psum x2, waiting for transfers between devices, shards(): hh = lax.psum(local_gram, ('row', 'col'))  203 us
    all_gather x2, blocking collectives, shards(): copies = lax.all_gather(hb, 'row', axis=0, tiled=True)  29.4 us
    psum x1, blocking collectives, shards(): col_sum, grand = lax.psum((jnp.sum(kern, axis=0), band), 'row')  15.4 us
    all_gather x1, blocking collectives, shards(): row_pts = lax.all_gather(points, 'col', axis=0, tiled=True)  11.9 us
    psum x1, blocking collectives, shards(): row_sum, band = lax.psum((jnp.sum(kern, axis=1), jnp.sum(kern)), 'col')  9.6 us
  transfers between devices with their start and end apart: 5, of which 2 were waited for; matrix products, arithmetic and copies ran while one was open for 3% of the time, Pallas kernels for 0%

commit v1 on v0

--- a/solution.py
+++ b/solution.py
@@ -41,7 +41,8 @@
         local_gram = lax.dot_general(
             h, h, (((0,), (0,)), ((), ())), precision=lax.Precision.HIGHEST
         )
-        hh = lax.psum(local_gram, ("row", "col"))
+        parts = lax.all_gather(local_gram, ("row", "col"))
+        hh = jnp.sum(parts, axis=0)
         scale = 0.5 / jnp.sqrt(jnp.sum(hh * hh) + 1e-06)
         h = jnp.maximum(h - scale * (jnp.dot(h, hh, precision=lax.Precision.HIGHEST) - ah), 0.0)
     return h / unit

time: 301 us -> 254 us (0.84)
  waiting for transfers between devices: 203 us -> 150 us
  other arithmetic: 5.03 us -> 11.7 us
    psum x2 -> x0, waiting for transfers between devices: 203 us -> none  [shards(): hh = lax.psum(local_gram, ('row', 'col'))]
    all_gather x0 -> x2, waiting for transfers between devices: none -> 108 us  [shards(): parts = lax.all_gather(local_gram, ('row', 'col'))]
    reduce_scatter x2, waiting for transfers between devices: 0.04 us -> 40.8 us  [shards(): lax.psum_scatter(jnp.dot(affinity, copies, preferred_element_type=jnp.flo...]
    reduce_sum x0 -> x2, other arithmetic: none -> 7.86 us  [shards(): hh = jnp.sum(parts, axis=0)]
  transfers between devices with their start and end apart: 5 -> 5, of which waited for: 2 -> 4; matrix products, arithmetic and copies ran while one was open for 3% -> 7% of each run, Pallas kernels for 0% -> 0%
where the time goes in v1:
time: 254 us
  waiting for transfers between devices  150 us (59%)
  blocking collectives  66.5 us (26%)
  between operations  15.2 us (6%)
  other arithmetic  11.7 us (5%)
  matrix products  10.4 us (4%)
    all_gather x2, waiting for transfers between devices, shards(): parts = lax.all_gather(local_gram, ('row', 'col'))  108 us
    reduce_scatter x2, waiting for transfers between devices, shards(): lax.psum_scatter(jnp.dot(affinity, copies, preferred_element_type=jnp.flo...  40.8 us
    all_gather x2, blocking collectives, shards(): copies = lax.all_gather(hb, 'row', axis=0, tiled=True)  29.6 us
    psum x1, blocking collectives, shards(): col_sum, grand = lax.psum((jnp.sum(kern, axis=0), band), 'row')  15.5 us
    all_gather x1, blocking collectives, shards(): row_pts = lax.all_gather(points, 'col', axis=0, tiled=True)  11.9 us
    psum x1, blocking collectives, shards(): row_sum, band = lax.psum((jnp.sum(kern, axis=1), jnp.sum(kern)), 'col')  9.65 us
    reduce_sum x2, other arithmetic, shards(): hh = jnp.sum(parts, axis=0)  7.86 us
  transfers between devices with their start and end apart: 5, of which 4 were waited for; matrix products, arithmetic and copies ran while one was open for 7% of the time, Pallas kernels for 0%

profile of v1, /device:TPU:0, one launch (start us, length us, event | category | flops | bytes accessed | tf_op | source)
XLA Modules:
  0.0 253.8 jit_solution(12780438340869378497)
XLA Ops:
  6.5 0.7 all-gather.6.cloned.1.call-update
  7.3 0.0 all-gather.8.cloned.1.call-start
  7.3 2.0 fusion.12
  9.3 0.0 all-gather.8.cloned.1.call-update
  9.4 0.0 reduce-scatter.3.cloned.1.call-start
  9.4 11.9 %all_gather.26 = bf16[256,1024]{1,0:T(8,128)(2,1)S(1)} all-gather(bf16[64,1024]{1,0:T(8,128)(2,1)} %param.2), channel_id=1, replica_groups=mesh['row'=8,'col'=4] {'col'}, dimensions={0}, use_global_device_ids=true | all-gather | bytes 655360 | tf_op jit(solution)/shard_map/all_gather | solution.py:17
  21.3 0.8 multiply_convert_fusion
  22.1 15.2 %all_gather.28 = bf16[512,256]{1,0:T(8,128)(2,1)S(1)} all-gather(bf16[64,256]{1,0:T(8,128)(2,1)S(1)} %multiply_convert_fusion), channel_id=1, replica_groups=mesh['row'=8,'col'=4] {'row'}, dimensions={0}, use_global_device_ids=true | all-gather | bytes 294912 | tf_op jit(solution)/shard_map/all_gather | solution.py:34
  37.4 0.2 multiply_reduce_fusion.1
  37.5 0.0 all-gather.6.cloned.1.call-done
  37.6 1.5 multiply_reduce_fusion
  39.1 2.5 fusion.20
  41.5 9.6 %all-reduce.1 = (f32[]{:T(128)}, f32[256]{0:T(256)S(1)}) all-reduce(f32[]{:T(128)} %get-tuple-element.6, f32[256]{0:T(256)S(1)} %get-tuple-element.5), channel_id=1, replica_groups=mesh['row'=8,'col'=4] {'col'}, use_global_device_ids=true, to_apply=%region_9.0 | all-reduce | flops 257 | bytes 2056 | tf_op jit(solution)/shard_map/psum | solution.py:25
  51.2 15.5 %all-reduce = (f32[]{:T(128)}, f32[512]{0:T(512)S(1)}) all-reduce(f32[]{:T(128)} %get-tuple-element.10, f32[512]{0:T(512)S(1)} %get-tuple-element.7), channel_id=1, replica_groups=mesh['row'=8,'col'=4] {'row'}, use_global_device_ids=true, to_apply=%region_10.0 | all-reduce | flops 513 | bytes 4104 | tf_op jit(solution)/shard_map/psum | solution.py:26
  67.3 1.0 fusion.19
  68.3 0.0 reduce-scatter.3.cloned.1.call-update
  68.3 0.0 all-gather.10.cloned.1.call-start
  68.4 46.1 %all-gather.8.cloned.1.call-done = f32[8192,256]{1,0:T(8,128)} async-done(((f32[256,256]{1,0:T(8,128)}), f32[8192,256]{1,0:T(8,128)}) %all-gather.8.cloned.1.call-update) | async-done | bytes 8388624 | tf_op jit(solution)/shard_map/all_gather | solution.py:44
  114.5 3.9 %reduce_sum.81 = f32[256,256]{1,0:T(8,128)S(1)} reduce(f32[32,256,256]{2,1,0:T(8,128)} %bitcast.11, f32[]{:T(128)} %constant.4.clone.1), dimensions={0}, to_apply=%region_0.0 | reduce | flops 2031616 | bytes 8650756 | tf_op jit(solution)/shard_map/reduce_sum | solution.py:45
  118.4 0.7 multiply_reduce_fusion.3
  119.8 20.5 %reduce-scatter.3.cloned.1.call-done = f32[64,256]{1,0:T(8,128)} async-done(((f32[256,256]{1,0:T(8,128)}), f32[64,256]{1,0:T(8,128)}) %reduce-scatter.3.cloned.1.call-update) | async-done | bytes 65552 | tf_op jit(solution)/shard_map/reduce_scatter | solution.py:35
  140.3 1.1 fusion.21
  141.4 1.1 fusion.22
  142.5 0.0 all-gather.10.cloned.1.call-update
  142.5 0.0 reduce-scatter.5.cloned.1.call-start
  142.6 14.4 %all_gather.31 = bf16[512,256]{1,0:T(8,128)(2,1)S(1)} all-gather(bf16[64,256]{1,0:T(8,128)(2,1)S(1)} %get-tuple-element.13), channel_id=1, replica_groups=mesh['row'=8,'col'=4] {'row'}, dimensions={0}, use_global_device_ids=true | all-gather | bytes 294912 | tf_op jit(solution)/shard_map/all_gather | solution.py:34
  156.9 1.0 fusion.18
  157.9 62.0 %all-gather.10.cloned.1.call-done = f32[8192,256]{1,0:T(8,128)} async-done(((f32[256,256]{1,0:T(8,128)}), f32[8192,256]{1,0:T(8,128)}) %all-gather.10.cloned.1.call-update) | async-done | bytes 8388624 | tf_op jit(solution)/shard_map/all_gather | solution.py:44
  220.0 3.9 %reduce_sum.88 = f32[256,256]{1,0:T(8,128)S(1)} reduce(f32[32,256,256]{2,1,0:T(8,128)} %bitcast.12, f32[]{:T(128)} %constant.4.clone.1), dimensions={0}, to_apply=%region_12.0 | reduce | flops 2031616 | bytes 8650756 | tf_op jit(solution)/shard_map/reduce_sum | solution.py:45
  223.9 0.7 multiply_reduce_fusion.2
  225.2 20.3 %reduce-scatter.5.cloned.1.call-done = f32[64,256]{1,0:T(8,128)} async-done(((f32[256,256]{1,0:T(8,128)}), f32[64,256]{1,0:T(8,128)}) %reduce-scatter.5.cloned.1.call-update) | async-done | bytes 65552 | tf_op jit(solution)/shard_map/reduce_scatter | solution.py:35
  245.6 1.7 fusion.7
  (6 shorter events, 0.0 us)
Async XLA Ops:
  6.5 133.7 %copy-start = (f32[64,256]{1,0:T(8,128)S(1)}, f32[64,256]{1,0:T(8,128)}, u32[]{:S(2)}) copy-start(f32[64,256]{1,0:T(8,128)} %param.3) | copy-start | bytes 196612
  6.5 31.0 %all-gather.6.cloned.1.call-start = ((), (), s32[]{:S(2)}) async-start(), calls=%async_computation.2 | async-start | bytes 1179648 | tf_op jit(solution)/shard_map/all_gather | solution.py:18
  7.3 107.3 %all-gather.8.cloned.1.call-start = ((), (), s32[]{:S(2)}) async-start(), calls=%async_computation.5 | async-start | bytes 8650752 | tf_op jit(solution)/shard_map/all_gather | solution.py:44
  9.4 130.9 %reduce-scatter.3.cloned.1.call-start = ((), (), s32[]{:S(2)}) async-start(), calls=%async_computation.3 | async-start | bytes 327680 | tf_op jit(solution)/shard_map/reduce_scatter | solution.py:35
  68.3 151.6 %all-gather.10.cloned.1.call-start = ((), (), s32[]{:S(2)}) async-start(), calls=%async_computation.6 | async-start | bytes 8650752 | tf_op jit(solution)/shard_map/all_gather | solution.py:44
  142.5 103.0 %reduce-scatter.5.cloned.1.call-start = ((), (), s32[]{:S(2)}) async-start(), calls=%async_computation.4 | async-start | bytes 327680 | tf_op jit(solution)/shard_map/reduce_scatter | solution.py:35
Sparse Core Ops, SparseCore 0:
  8.9 26.0 all-gather.5
  37.9 76.6 all-gather.7
  117.3 22.9 reduce-scatter.2
  143.0 76.9 all-gather.9
  222.6 22.9 reduce-scatter.4
